TPU v7x, 128 devices: a whole 4x4x4 slice. The times are simulated.
128 devices in a mesh: variant: 8 (over z_lo, x), vocab: 16 (over y, z_hi, core).
Axes of the slice: x: 4, y: 4, z: 4 (z_hi: 2, z_lo: 2; z = z_hi * 2 + z_lo), core: 2. Of those that a mesh axis runs over, the one named last changes fastest.
Arguments:
- teacher_hidden: bfloat16 [8, 256, 4096], P(None, None, ('variant', 'vocab')), may hold values from -24 to 24
- teacher_weight: bfloat16 [4096, 64128], P(None, ('vocab', 'variant')), may hold values from -1 to 1
- variant_ids: int32 [8], replicated, may hold values from 0 to 13
- temps: float32 [14], replicated, may hold values from 0.7 to 1.5
- student_hidden: bfloat16 [256, 2048], P(None, 'variant'), may hold values from -24 to 24
- student_weight: bfloat16 [2048, 64128], P('variant', 'vocab'), may hold values from -1 to 1
- token_ids: int32 [256], P('variant'), may hold values from 0 to 64127
- loss_mask: int32 [256], P('variant'), may hold values 0 or 1
Outputs:
- token_loss: float32 [256], P('variant')
- student_grad: float32 [2048, 64128], P('variant', 'vocab')
All inputs are finite; a program needn't handle non-finite values. No bound on the sum of `loss_mask` on one device may be relied on, other than what follows from the above.
Results may differ from a plain program's by a relative error of at most 0.0025.
Values may be sent and summed in bfloat16 or wider, within the bound.
No kernel may reach another device: no remote copies, remote signals or barrier semaphores. Data moves between devices by JAX's collectives and lax.ppermute only.
A program may use at most 192 MiB of HBM per device.

v0:
```python
import jax
import jax.numpy as jnp
from jax import lax
from jax.sharding import PartitionSpec as P

mix_weight = 0.5
loss_scale = 4096.0


def on_device(
    teacher_hidden,
    teacher_weight,
    variant_ids,
    temps,
    student_hidden,
    student_weight,
    token_ids,
    loss_mask,
):
    n_variant = lax.axis_size("variant")
    categories = jnp.arange(temps.shape[0], dtype=jnp.int32)
    taus = jnp.sum(
        jnp.where(variant_ids[:, None] == categories[None, :], temps[None, :], 0.0), axis=1
    )
    hidden_all = lax.all_gather(teacher_hidden, ("variant", "vocab"), axis=2, tiled=True)
    scaled = (
        jnp.einsum("vtd,dc->vtc", hidden_all, teacher_weight, preferred_element_type=jnp.float32)
        / taus[:, None, None]
    )
    local_max = jnp.max(scaled, axis=2)
    top = lax.pmax(local_max, ("variant", "vocab"))
    total = lax.psum(jnp.sum(jnp.exp(scaled - top[:, :, None]), axis=2), ("variant", "vocab"))
    probs = jnp.exp(scaled - top[:, :, None]) / total[:, :, None]
    averaged_cols = jnp.sum(probs, axis=0) / n_variant
    averaged = lax.all_to_all(
        averaged_cols.astype(jnp.bfloat16), "variant", split_axis=0, concat_axis=1, tiled=True
    ).astype(averaged_cols.dtype)
    block = student_hidden
    logits = lax.psum_scatter(
        jnp.dot(block, student_weight, preferred_element_type=jnp.float32),
        "variant",
        scatter_dimension=0,
        tiled=True,
    )
    local_max = jnp.max(logits, axis=1)
    top = lax.pmax(local_max, "vocab")
    total = lax.psum(jnp.sum(jnp.exp(logits - top[:, None]), axis=1), "vocab")
    log_probs = logits - (top + jnp.log(total))[:, None]
    probs_student = jnp.exp(log_probs)
    columns = lax.axis_index("vocab") * logits.shape[1] + jnp.arange(
        logits.shape[1], dtype=jnp.int32
    )
    onehot = token_ids[:, None] == columns[None, :]
    soft, hard = lax.psum(
        (jnp.sum(averaged * log_probs, axis=1), jnp.sum(jnp.where(onehot, log_probs, 0.0), axis=1)),
        "vocab",
    )
    maskf = loss_mask.astype(jnp.float32)
    token_loss = maskf * (-mix_weight * soft - (1.0 - mix_weight) * hard)
    error = (
        loss_scale
        * maskf[:, None]
        * (probs_student - mix_weight * averaged - (1.0 - mix_weight) * onehot.astype(jnp.float32))
    ).astype(jnp.bfloat16)
    block = student_hidden
    student_grad = lax.dot_general(
        block,
        lax.all_gather(error, "variant", axis=0, tiled=True),
        (((0,), (0,)), ((), ())),
        preferred_element_type=jnp.float32,
    )
    return (token_loss, student_grad)


def solution(mesh):
    in_specs = (
        P(None, None, ("variant", "vocab")),
        P(None, ("vocab", "variant")),
        P(),
        P(),
        P(None, "variant"),
        P("variant", "vocab"),
        P("variant"),
        P("variant"),
    )
    out_specs = (P("variant"), P("variant", "vocab"))
    return jax.shard_map(
        on_device, mesh=mesh, in_specs=in_specs, out_specs=out_specs, check_vma=False
    )
```

profile of v0, /device:TPU:0, one launch (start us, length us, event | category | flops | bytes accessed | tf_op | source)
XLA Modules:
  0.0 505.8 jit_solution(16824957268856968234)
XLA Ops:
  8.0 0.0 copy-start
  8.0 0.0 copy-start.5
  8.0 0.0 copy-start.6
  8.0 0.0 copy-start.4
  8.0 0.0 reduce-scatter.2.cloned.1.call-start
  8.1 1.5 copy-done
  9.6 3.6 fusion.11
  13.2 0.0 reduce-scatter.2.cloned.1.call-update
  13.2 0.0 all-gather.3.cloned.1.call-start
  13.2 0.5 all-gather.3.cloned.1.call-update
  13.8 0.0 copy-done.5
  13.8 0.0 copy-done.6
  13.8 0.2 select_reduce_fusion
  14.0 0.0 copy-done.4
  14.0 60.6 %reduce-scatter.2.cloned.1.call-done = f32[32,4008]{1,0:T(8,128)} async-done(((f32[256,4008]{1,0:T(8,128)}), f32[32,4008]{1,0:T(8,128)}) %reduce-scatter.2.cloned.1.call-update) | async-done | bytes 513040 | tf_op jit(solution)/shard_map/reduce_scatter | solution.py:39
  74.6 1.2 reduce_max.19
  75.8 38.9 %pmax.15 = f32[32]{0:T(128)S(1)} all-reduce(f32[32]{0:T(128)S(1)} %reduce_max.19), channel_id=1, replica_groups=mesh['variant'=8,'vocab'=16] {'vocab'}, use_global_device_ids=true, to_apply=%region_8.9 | all-reduce | flops 32 | bytes 256 | tf_op jit(solution)/shard_map/pmax | solution.py:46
  114.7 151.1 %all-gather.3.cloned.1.call-done = bf16[8,256,4096]{1,2,0:T(8,128)(2,1)} async-done(((bf16[8,256,32]{1,2,0:T(8,128)(2,1)}), bf16[8,256,4096]{1,2,0:T(8,128)(2,1)}) %all-gather.3.cloned.1.call-update) | async-done | bytes 16777232 | tf_op jit(solution)/shard_map/all_gather | solution.py:25
  265.9 14.8 %fusion.10 = (f32[8,256]{1,0:T(8,128)S(1)}, f32[8,256,501]{1,2,0:T(8,128)}) fusion(f32[8]{0:T(128)S(1)} %select_reduce_fusion, bf16[8,256,4096]{1,2,0:T(8,128)(2,1)} %all-gather.3.cloned.1.call-done, bf16[4096,501]{0,1:T(8,128)(2,1)} %param.9), kind=kOutput, calls=%fused_computation.23 | convolution fusion | flops 8407435264 | bytes 24993824 | tf_op jit(solution)/shard_map/vtd,dc->vtc/dot_general | solution.py:27
  280.6 62.0 %pmax.14 = f32[8,256]{1,0:T(8,128)S(1)} all-reduce(f32[8,256]{1,0:T(8,128)S(1)} %get-tuple-element.7), channel_id=1, replica_groups=mesh['variant'=8,'vocab'=16] {'variant','vocab'}, use_global_device_ids=true, to_apply=%region_2.3 | all-reduce | flops 2048 | bytes 16384 | tf_op jit(solution)/shard_map/pmax | solution.py:31
  342.6 2.7 fusion.2
  345.4 0.0 copy-start.1
  345.4 64.6 %psum.28 = f32[8,256]{1,0:T(8,128)S(1)} all-reduce(f32[8,256]{1,0:T(8,128)S(1)} %fusion.2), channel_id=1, replica_groups=mesh['variant'=8,'vocab'=16] {'variant','vocab'}, use_global_device_ids=true, to_apply=%region_4.5 | all-reduce | flops 2048 | bytes 16384 | tf_op jit(solution)/shard_map/psum | solution.py:32
  410.0 0.0 copy-start.3
  410.0 2.9 divide_reduce_fusion
  412.9 0.0 copy-start.2
  413.0 0.8 copy.13
  413.8 3.4 all-to-all-start
  417.3 0.0 all-gather.5.cloned.1.call-start
  417.3 0.0 copy-done.1
  417.3 0.3 exponential_reduce_fusion
  417.6 34.1 %psum.29 = f32[32]{0:T(128)S(1)} all-reduce(f32[32]{0:T(128)S(1)} %exponential_reduce_fusion), channel_id=1, replica_groups=mesh['variant'=8,'vocab'=16] {'vocab'}, use_global_device_ids=true, to_apply=%region_10.11 | all-reduce | flops 32 | bytes 256 | tf_op jit(solution)/shard_map/psum | solution.py:47
  451.7 0.0 all-to-all-done
  451.7 0.1 convert_bitcast_fusion
  451.8 1.1 copy.14
  452.9 1.4 reshape.27
  454.2 0.0 copy-done.3
  454.2 1.1 multiply_reduce_fusion
  455.4 0.0 all-gather.5.cloned.1.call-update
  455.4 33.7 %all-reduce = (f32[32]{0:T(128)S(1)}, f32[32]{0:T(128)S(1)}) all-reduce(f32[32]{0:T(128)S(1)} %get-tuple-element.3, f32[32]{0:T(128)S(1)} %get-tuple-element.2), channel_id=1, replica_groups=mesh['variant'=8,'vocab'=16] {'vocab'}, use_global_device_ids=true, to_apply=%region_14.15 | all-reduce | flops 64 | bytes 512 | tf_op jit(solution)/shard_map/psum | solution.py:54
  489.1 0.5 subtract_multiply_fusion
  489.6 4.4 all-gather.5.cloned.1.call-done
  494.0 0.0 copy-done.2
  494.0 4.3 convolution_bitcast_fusion
  (4 shorter events, 0.1 us)
Async XLA Ops:
  8.0 1.6 copy-start
  8.0 5.8 %copy-start.5 = (f32[14]{0:T(128)S(1)}, f32[14]{0:T(128)}, u32[]{:S(2)}) copy-start(f32[14]{0:T(128)} %param.11) | copy-start | bytes 172
  8.0 5.8 %copy-start.6 = (s32[8]{0:T(128)S(1)}, s32[8]{0:T(128)}, u32[]{:S(2)}) copy-start(s32[8]{0:T(128)} %param.10) | copy-start | bytes 100
  8.0 5.9 %copy-start.4 = (s32[32]{0:T(128)S(1)}, s32[32]{0:T(128)}, u32[]{:S(2)}) copy-start(s32[32]{0:T(128)} %param.15) | copy-start | bytes 388
  8.0 66.6 %reduce-scatter.2.cloned.1.call-start = ((), (), s32[]{:S(2)}) async-start(), calls=%async_computation.3 | async-start | bytes 4718592 | tf_op jit(solution)/shard_map/reduce_scatter | solution.py:39
  13.2 252.7 %all-gather.3.cloned.1.call-start = ((), (), s32[]{:S(2)}) async-start(), calls=%async_computation.2 | async-start | bytes 16908288 | tf_op jit(solution)/shard_map/all_gather | solution.py:25
  345.4 71.9 %copy-start.1 = (f32[32,4008]{1,0:T(8,128)S(1)}, f32[32,4008]{1,0:T(8,128)}, u32[]{:S(2)}) copy-start(f32[32,4008]{1,0:T(8,128)} %reduce-scatter.2.cloned.1.call-done) | copy-start | bytes 1539076
  410.0 44.2 %copy-start.3 = (s32[32]{0:T(128)S(1)}, s32[32]{0:T(128)}, u32[]{:S(2)}) copy-start(s32[32]{0:T(128)} %param.14) | copy-start | bytes 388
  412.9 81.1 %copy-start.2 = (bf16[256,256]{1,0:T(8,128)(2,1)S(1)}, bf16[256,256]{1,0:T(8,128)(2,1)}, u32[]{:S(2)}) copy-start(bf16[256,256]{1,0:T(8,128)(2,1)} %param.12) | copy-start | bytes 393220
  413.8 37.9 %all-to-all-start = ((bf16[8,32,501]{2,1,0:T(8,128)(2,1)}), bf16[8,32,501]{2,1,0:T(8,128)(2,1)S(1)}, u32[]{:S(2)}, u32[]{:S(2)}) async-start(bf16[8,32,501]{2,1,0:T(8,128)(2,1)} %bitcast.1), calls=%async_computation | async-start | bytes 524288 | tf_op jit(solution)/shard_map/all_to_all | solution.py:35
  417.3 76.8 %all-gather.5.cloned.1.call-start = ((), (), s32[]{:S(2)}) async-start(), calls=%async_computation.4 | async-start | bytes 2359296 | tf_op jit(solution)/shard_map/all_gather | solution.py:68
Sparse Core Ops, SparseCore 0:
  13.3 61.2 reduce-scatter.1
  455.5 38.4 all-gather.4
Sparse Core Ops, SparseCore 1:
  15.4 250.4 all-gather.2
where the time goes:
time: 506 us
  blocking collectives  233 us (46%)
  waiting for transfers between devices  217 us (43%)
  matrix products  22.7 us (4%)
  between operations  15.6 us (3%)
  other arithmetic  9.06 us (2%)
    all_gather x1, waiting for transfers between devices, on_device(): lax.all_gather(teacher_hidden, ('variant', 'vocab'), axis=2, tiled=True)  151 us
    psum x1, blocking collectives, on_device(): lax.psum(jnp.sum(jnp.exp(scaled - top[:, :, None]), axis=2), ('variant',...  64.6 us
    pmax x1, blocking collectives, on_device(): top = lax.pmax(local_max, ('variant', 'vocab'))  62 us
    reduce_scatter x1, waiting for transfers between devices, on_device(): lax.psum_scatter(jnp.dot(block, student_weight, preferred_element_type=jn...  60.6 us
    pmax x1, blocking collectives, on_device(): top = lax.pmax(local_max, 'vocab')  38.9 us
    psum x1, blocking collectives, on_device(): total = lax.psum(jnp.sum(jnp.exp(logits - top[:, None]), axis=1), 'vocab')  34.1 us
    psum x1, blocking collectives, on_device(): lax.psum((jnp.sum(averaged * log_probs, axis=1), jnp.sum(jnp.where(onehot...  33.7 us
    dot_general x1, matrix products, on_device(): jnp.einsum('vtd,dc->vtc', hidden_all, teacher_weight, preferred_element_t...  14.8 us
  transfers between devices with their start and end apart: 4, of which 3 were waited for; matrix products, arithmetic and copies ran while one was open for 0% of the time, Pallas kernels for 0%

commit v1 on v0

--- a/solution.py
+++ b/solution.py
@@ -29,7 +29,9 @@
     )
     local_max = jnp.max(scaled, axis=2)
     top = lax.pmax(local_max, ("variant", "vocab"))
-    total = lax.psum(jnp.sum(jnp.exp(scaled - top[:, :, None]), axis=2), ("variant", "vocab"))
+    total = lax.psum(
+        lax.psum(jnp.sum(jnp.exp(scaled - top[:, :, None]), axis=2), "vocab"), "variant"
+    )
     probs = jnp.exp(scaled - top[:, :, None]) / total[:, :, None]
     averaged_cols = jnp.sum(probs, axis=0) / n_variant
     averaged = lax.all_to_all(

time: 506 us -> 467 us (0.923)
  blocking collectives: 233 us -> 189 us
    psum x2, blocking collectives: 98.7 us -> 54.1 us  [the longest x1 37 us: on_device(): lax.psum(jnp.sum(jnp.exp(scaled - top[:, :, None]), axis=2), 'vocab')]
    all_to_all x1, waiting for transfers between devices: 0.01 us -> 7.14 us  [on_device(): lax.all_to_all(averaged_cols.astype(jnp.bfloat16), 'variant', split_axis=...]
  transfers between devices with their start and end apart: 4 -> 4, of which waited for: 3 -> 4; matrix products, arithmetic and copies ran while one was open for 0% -> 1% of each run, Pallas kernels for 0% -> 0%
where the time goes in v1:
time: 467 us; the launch traced here: 466 us
  waiting for transfers between devices  221 us (47%)
  blocking collectives  189 us (40%)
  matrix products  22.7 us (5%)
  between operations  15.6 us (3%)
  other arithmetic  10.1 us (2%)
  local copies, waits for them, and re-layouts  4.83 us (1%)
    all_gather x1, waiting for transfers between devices, on_device(): lax.all_gather(teacher_hidden, ('variant', 'vocab'), axis=2, tiled=True)  150 us
    pmax x1, blocking collectives, on_device(): top = lax.pmax(local_max, ('variant', 'vocab'))  62.3 us
    reduce_scatter x1, waiting for transfers between devices, on_device(): lax.psum_scatter(jnp.dot(block, student_weight, preferred_element_type=jn...  60.6 us
    pmax x1, blocking collectives, on_device(): top = lax.pmax(local_max, 'vocab')  38.9 us
    psum x1, blocking collectives, on_device(): lax.psum(jnp.sum(jnp.exp(scaled - top[:, :, None]), axis=2), 'vocab')  37 us
    psum x1, blocking collectives, on_device(): lax.psum((jnp.sum(averaged * log_probs, axis=1), jnp.sum(jnp.where(onehot...  33.5 us
    psum x1, blocking collectives, on_device(): lax.psum(lax.psum(jnp.sum(jnp.exp(scaled - top[:, :, None]), axis=2), 'vo...  17.2 us
    dot_general x1, matrix products, on_device(): jnp.einsum('vtd,dc->vtc', hidden_all, teacher_weight, preferred_element_t...  14.8 us
  transfers between devices with their start and end apart: 4, of which 4 were waited for; matrix products, arithmetic and copies ran while one was open for 1% of the time, Pallas kernels for 0%

profile of v1, /device:TPU:0, one launch (start us, length us, event | category | flops | bytes accessed | tf_op | source)
XLA Modules:
  0.0 466.1 jit_solution(10442143256348705874)
XLA Ops:
  8.0 0.0 copy-start
  8.0 0.0 copy-start.5
  8.0 0.0 copy-start.6
  8.0 0.0 copy-start.4
  8.0 0.0 reduce-scatter.2.cloned.1.call-start
  8.1 1.5 copy-done
  9.6 3.6 fusion.11
  13.2 0.0 reduce-scatter.2.cloned.1.call-update
  13.2 0.0 all-gather.3.cloned.1.call-start
  13.2 0.5 all-gather.3.cloned.1.call-update
  13.8 0.0 copy-done.5
  13.8 0.0 copy-done.6
  13.8 0.2 select_reduce_fusion
  14.0 0.0 copy-done.4
  14.0 60.6 %reduce-scatter.2.cloned.1.call-done = f32[32,4008]{1,0:T(8,128)} async-done(((f32[256,4008]{1,0:T(8,128)}), f32[32,4008]{1,0:T(8,128)}) %reduce-scatter.2.cloned.1.call-update) | async-done | bytes 513040 | tf_op jit(solution)/shard_map/reduce_scatter | solution.py:41
  74.6 1.2 reduce_max.19
  75.8 38.9 %pmax.15 = f32[32]{0:T(128)S(1)} all-reduce(f32[32]{0:T(128)S(1)} %reduce_max.19), channel_id=1, replica_groups=mesh['variant'=8,'vocab'=16] {'vocab'}, use_global_device_ids=true, to_apply=%region_9.10 | all-reduce | flops 32 | bytes 256 | tf_op jit(solution)/shard_map/pmax | solution.py:48
  114.7 1.3 exponential_reduce_fusion
  116.0 149.5 %all-gather.3.cloned.1.call-done = bf16[8,256,4096]{1,2,0:T(8,128)(2,1)} async-done(((bf16[8,256,32]{1,2,0:T(8,128)(2,1)}), bf16[8,256,4096]{1,2,0:T(8,128)(2,1)}) %all-gather.3.cloned.1.call-update) | async-done | bytes 16777232 | tf_op jit(solution)/shard_map/all_gather | solution.py:25
  265.5 14.8 %fusion.10 = (f32[8,256]{1,0:T(8,128)S(1)}, f32[8,256,501]{1,2,0:T(8,128)}) fusion(f32[8]{0:T(128)S(1)} %select_reduce_fusion, bf16[8,256,4096]{1,2,0:T(8,128)(2,1)} %all-gather.3.cloned.1.call-done, bf16[4096,501]{0,1:T(8,128)(2,1)} %param.9), kind=kOutput, calls=%fused_computation.23 | convolution fusion | flops 8407435264 | bytes 24993824 | tf_op jit(solution)/shard_map/vtd,dc->vtc/dot_general | solution.py:27
  280.3 62.3 %pmax.14 = f32[8,256]{1,0:T(8,128)S(1)} all-reduce(f32[8,256]{1,0:T(8,128)S(1)} %get-tuple-element.9), channel_id=1, replica_groups=mesh['variant'=8,'vocab'=16] {'variant','vocab'}, use_global_device_ids=true, to_apply=%region_2.3 | all-reduce | flops 2048 | bytes 16384 | tf_op jit(solution)/shard_map/pmax | solution.py:31
  342.6 2.7 fusion.2
  345.3 37.0 %all-reduce.1 = (f32[8,256]{1,0:T(8,128)S(1)}, f32[32]{0:T(128)S(1)}) all-reduce(f32[8,256]{1,0:T(8,128)S(1)} %fusion.2, f32[32]{0:T(128)S(1)} %exponential_reduce_fusion), channel_id=1, replica_groups=mesh['variant'=8,'vocab'=16] {'vocab'}, use_global_device_ids=true, to_apply=%region_4.5 | all-reduce | flops 2080 | bytes 16640 | tf_op jit(solution)/shard_map/psum | solution.py:33
  382.3 17.2 %psum.36 = f32[8,256]{1,0:T(8,128)S(1)} all-reduce(f32[8,256]{1,0:T(8,128)S(1)} %get-tuple-element.6), channel_id=1, replica_groups=mesh['variant'=8,'vocab'=16] {'variant'}, use_global_device_ids=true, to_apply=%region_5.6 | all-reduce | flops 2048 | bytes 16384 | tf_op jit(solution)/shard_map/psum | solution.py:32
  399.4 0.0 copy-start.1
  399.5 0.0 copy-start.3
  399.5 3.0 divide_reduce_fusion
  402.4 0.0 copy-start.2
  402.5 0.8 copy.13
  403.4 3.4 all-to-all-start
  406.8 0.0 all-gather.5.cloned.1.call-start
  406.9 7.1 %all-to-all-done = bf16[8,32,501]{2,1,0:T(8,128)(2,1)S(1)} async-done(((bf16[8,32,501]{2,1,0:T(8,128)(2,1)}), bf16[8,32,501]{2,1,0:T(8,128)(2,1)S(1)}, u32[]{:S(2)}, u32[]{:S(2)}) %all-to-all-start) | async-done | bytes 256544 | tf_op jit(solution)/shard_map/all_to_all | solution.py:37
  414.0 0.1 convert_bitcast_fusion
  414.1 1.1 copy.14
  415.2 1.4 reshape.27
  416.5 0.0 copy-done.1
  416.5 0.0 copy-done.3
  416.5 1.1 multiply_reduce_fusion
  417.6 0.0 all-gather.5.cloned.1.call-update
  417.7 33.5 %all-reduce = (f32[32]{0:T(128)S(1)}, f32[32]{0:T(128)S(1)}) all-reduce(f32[32]{0:T(128)S(1)} %get-tuple-element.3, f32[32]{0:T(128)S(1)} %get-tuple-element.2), channel_id=1, replica_groups=mesh['variant'=8,'vocab'=16] {'vocab'}, use_global_device_ids=true, to_apply=%region_15.16 | all-reduce | flops 64 | bytes 512 | tf_op jit(solution)/shard_map/psum | solution.py:56
  451.1 0.5 subtract_multiply_fusion
  451.7 2.7 all-gather.5.cloned.1.call-done
  454.3 0.0 copy-done.2
  454.3 4.3 convolution_bitcast_fusion
  (4 shorter events, 0.1 us)
Async XLA Ops:
  8.0 1.6 copy-start
  8.0 5.7 %copy-start.5 = (f32[14]{0:T(128)S(1)}, f32[14]{0:T(128)}, u32[]{:S(2)}) copy-start(f32[14]{0:T(128)} %param.11) | copy-start | bytes 172
  8.0 5.7 %copy-start.6 = (s32[8]{0:T(128)S(1)}, s32[8]{0:T(128)}, u32[]{:S(2)}) copy-start(s32[8]{0:T(128)} %param.10) | copy-start | bytes 100
  8.0 5.9 %copy-start.4 = (s32[32]{0:T(128)S(1)}, s32[32]{0:T(128)}, u32[]{:S(2)}) copy-start(s32[32]{0:T(128)} %param.15) | copy-start | bytes 388
  8.0 66.6 %reduce-scatter.2.cloned.1.call-start = ((), (), s32[]{:S(2)}) async-start(), calls=%async_computation.3 | async-start | bytes 4718592 | tf_op jit(solution)/shard_map/reduce_scatter | solution.py:41
  13.2 252.4 %all-gather.3.cloned.1.call-start = ((), (), s32[]{:S(2)}) async-start(), calls=%async_computation.2 | async-start | bytes 16908288 | tf_op jit(solution)/shard_map/all_gather | solution.py:25
  399.4 17.1 %copy-start.1 = (f32[32,4008]{1,0:T(8,128)S(1)}, f32[32,4008]{1,0:T(8,128)}, u32[]{:S(2)}) copy-start(f32[32,4008]{1,0:T(8,128)} %reduce-scatter.2.cloned.1.call-done) | copy-start | bytes 1539076
  399.5 17.1 %copy-start.3 = (s32[32]{0:T(128)S(1)}, s32[32]{0:T(128)}, u32[]{:S(2)}) copy-start(s32[32]{0:T(128)} %param.14) | copy-start | bytes 388
  402.4 51.9 %copy-start.2 = (bf16[256,256]{1,0:T(8,128)(2,1)S(1)}, bf16[256,256]{1,0:T(8,128)(2,1)}, u32[]{:S(2)}) copy-start(bf16[256,256]{1,0:T(8,128)(2,1)} %param.12) | copy-start | bytes 393220
  403.4 10.6 %all-to-all-start = ((bf16[8,32,501]{2,1,0:T(8,128)(2,1)}), bf16[8,32,501]{2,1,0:T(8,128)(2,1)S(1)}, u32[]{:S(2)}, u32[]{:S(2)}) async-start(bf16[8,32,501]{2,1,0:T(8,128)(2,1)} %bitcast.1), calls=%async_computation | async-start | bytes 524288 | tf_op jit(solution)/shard_map/all_to_all | solution.py:37
  406.8 47.5 %all-gather.5.cloned.1.call-start = ((), (), s32[]{:S(2)}) async-start(), calls=%async_computation.4 | async-start | bytes 2359296 | tf_op jit(solution)/shard_map/all_gather | solution.py:70
Sparse Core Ops, SparseCore 0:
  13.3 61.2 reduce-scatter.1
  417.8 36.4 all-gather.4
Sparse Core Ops, SparseCore 1:
  15.4 250.1 all-gather.2
